TPU v7x, 32 devices: a whole 2x2x4 slice. The times are simulated.
32 devices in a mesh: pole: 4 (over y, x), row: 8 (over z, core).
Axes of the slice: x: 2, y: 2, z: 4, core: 2. Of those that a mesh axis runs over, the one named last changes fastest.
Arguments:
- basis: bfloat16 [32768, 128], P('row'), may hold values from -24 to 24
- inverses: bfloat16 [4, 64, 512, 512], P('pole', 'row'), may hold values from -1.5 to 1.5
- lower: bfloat16 [64, 512, 512], P('row'), may hold values from -0.03955078 to 0.03955078
- upper: bfloat16 [64, 512, 512], P('row'), may hold values from -0.03955078 to 0.03955078
- pole_weights: float32 [4], P('pole'), may hold values from 0.5 to 1.5
Outputs:
- new_basis: float32 [32768, 128], P(('row', 'pole'))
All inputs are finite; a program needn't handle non-finite values.
Results may differ from a plain program's by a relative error of at most 0.003.
Values may be sent and summed in bfloat16 or wider, within the bound.
A program may use at most 64 MiB of HBM per device.

v0:
```python
import jax
import jax.numpy as jnp
from jax import lax
from jax.sharding import PartitionSpec as P

SWEEPS = 4


def padded_2(value, sides, width):
    for axis, dim in sides:
        peers, length = (lax.axis_size(axis), value.shape[dim])
        up = [(i, (i + 1) % peers) for i in range(peers - 1)]
        down = [(j, i) for i, j in up]
        last = lax.slice_in_dim(value, length - width, length, axis=dim)
        initial = lax.slice_in_dim(value, 0, width, axis=dim)
        before = lax.ppermute(last, axis, up)
        after = lax.ppermute(initial, axis, down)
        value = jnp.concatenate([before, value, after], axis=dim)
    return value


def shards(basis, inverses, lower, upper, pole_weights):
    rows, width = basis.shape
    count = inverses.shape[1]
    size = inverses.shape[-1]
    inverse = inverses[0]
    blocks = basis.reshape(count, size, width)
    state = jnp.einsum("bij,bjk->bik", inverse, blocks, preferred_element_type=jnp.float32).astype(
        jnp.bfloat16
    )
    for sweep in range(SWEEPS):
        padded = padded_2(state.reshape(rows, width), (("row", 0),), size)
        padded = padded.reshape(count + 2, size, width)
        rhs = blocks.astype(jnp.float32)
        rhs = rhs + jnp.einsum(
            "bij,bjk->bik", lower, padded[:-2], preferred_element_type=jnp.float32
        )
        rhs = rhs + jnp.einsum(
            "bij,bjk->bik", upper, padded[2:], preferred_element_type=jnp.float32
        )
        state = jnp.einsum(
            "bij,bjk->bik", inverse, rhs.astype(jnp.bfloat16), preferred_element_type=jnp.float32
        ).astype(jnp.bfloat16)
    weighted = pole_weights[0] * state.reshape(rows, width).astype(jnp.float32)
    total_rows = rows * lax.axis_size("row")
    filtered = lax.psum(weighted, "pole")
    share = rows // lax.axis_size("pole")
    mine = lax.dynamic_slice_in_dim(filtered, lax.axis_index("pole") * share, share, 0)
    partial_gram = jnp.dot(filtered.T, filtered, precision=lax.Precision.HIGHEST)
    gram = lax.psum(partial_gram, "row")
    gram = gram / total_rows
    factor = jnp.linalg.cholesky(gram)
    solved = jax.scipy.linalg.solve_triangular(factor, mine.T, lower=True)
    return solved.T


def solution(mesh):
    return jax.shard_map(
        shards,
        mesh=mesh,
        in_specs=(
            P("row", None),
            P("pole", "row", None, None),
            P("row", None, None),
            P("row", None, None),
            P("pole"),
        ),
        out_specs=P(("row", "pole"), None),
        check_vma=False,
    )
```

profile of v0, /device:TPU:0, one launch (start us, length us, event | category | flops | bytes accessed | tf_op | source)
XLA Modules:
  0.0 268.5 jit_solution(1977090597358284194)
XLA Ops:
  6.5 3.8 %fusion.18 = bf16[8,512,128]{2,1,0:T(8,128)(2,1)S(1)} fusion(bf16[8,512,128]{2,1,0:T(8,128)(2,1)} %bitcast.142, bf16[1,8,512,512]{3,2,1,0:T(8,128)(2,1)} %param.6), kind=kOutput, calls=%fused_computation.23 | convolution fusion | flops 537395200 | bytes 6291456 | tf_op jit(solution)/shard_map/bij,bjk->bik/dot_general | solution.py:28
  10.4 2.4 collective-permute-start
  14.7 3.7 %collective-permute-done.1 = bf16[512,128]{1,0:T(8,128)(2,1)} collective-permute-done((bf16[512,128]{1,0:T(8,128)(2,1)S(1)}, bf16[512,128]{1,0:T(8,128)(2,1)}, u32[]{:S(2)}, u32[]{:S(2)}) %collective-permute-start.1) | collective-permute-done | bytes 131104 | tf_op jit(solution)/shard_map/ppermute | solution.py:17
  18.4 2.0 pad_maximum_fusion.6
  20.4 3.7 %fusion.50 = f32[8,128,512]{2,1,0:T(8,128)S(1)} fusion(bf16[8,512,128]{2,1,0:T(8,128)(2,1)S(1)} %bitcast.131, bf16[8,512,512]{2,1,0:T(8,128)(2,1)} %param.7), kind=kOutput, calls=%fused_computation.60 | convolution fusion | flops 536870912 | bytes 7340032 | tf_op jit(solution)/shard_map/bij,bjk->bik/dot_general | solution.py:35
  24.1 7.6 %fusion.41 = bf16[8,512,128]{1,2,0:T(8,128)(2,1)} fusion(bf16[1,8,512,512]{3,2,1,0:T(8,128)(2,1)} %param.6, bf16[8,512,128]{1,2,0:T(8,128)(2,1)S(1)} %copy.15, f32[8,128,512]{2,1,0:T(8,128)S(1)} %fusion.50, bf16[8,512,128]{2,1,0:T(8,128)(2,1)} %bitcast.138, bf16[8,512,512]{2,1,0:T(8,128)(2,1)} %param.8), kind=kOutput, calls=%fused_computation.30 | convolution fusion | flops 1076363264 | bytes 13631488 | tf_op jit(solution)/shard_map/bij,bjk->bik/dot_general | solution.py:41
  32.7 5.4 %collective-permute-start.2 = (bf16[512,128]{0,1:T(8,128)(2,1)S(1)}, bf16[512,128]{0,1:T(8,128)(2,1)S(1)}, u32[]{:S(2)}, u32[]{:S(2)}) collective-permute-start(bf16[512,128]{0,1:T(8,128)(2,1)S(1)} %get-tuple-element.16), channel_id=1, source_target_pairs={{0,1},{1,2},{2,3},{3,4},{4,5},{5,6},{6,7},{8,9},{9,10},{10,11},{11... | collective-permute-start | bytes 393224 | tf_op jit(solution)/shard_map/ppermute | solution.py:16
  39.4 1.6 copy.16
  42.6 3.7 %fusion.51 = f32[8,128,512]{2,1,0:T(8,128)S(1)} fusion(bf16[8,512,128]{2,1,0:T(8,128)(2,1)S(1)} %bitcast.132, bf16[8,512,512]{2,1,0:T(8,128)(2,1)} %param.7), kind=kOutput, calls=%fused_computation.61 | convolution fusion | flops 536870912 | bytes 7340032 | tf_op jit(solution)/shard_map/bij,bjk->bik/dot_general | solution.py:35
  46.3 7.6 %fusion.38 = bf16[8,512,128]{1,2,0:T(8,128)(2,1)} fusion(bf16[1,8,512,512]{3,2,1,0:T(8,128)(2,1)} %param.6, bf16[8,512,128]{1,2,0:T(8,128)(2,1)S(1)} %copy.15, f32[8,128,512]{2,1,0:T(8,128)S(1)} %fusion.51, bf16[8,512,128]{2,1,0:T(8,128)(2,1)} %bitcast.139, bf16[8,512,512]{2,1,0:T(8,128)(2,1)} %param.8), kind=kOutput, calls=%fused_computation.29 | convolution fusion | flops 1076363264 | bytes 13631488 | tf_op jit(solution)/shard_map/bij,bjk->bik/dot_general | solution.py:41
  55.0 5.0 %collective-permute-start.4 = (bf16[512,128]{0,1:T(8,128)(2,1)S(1)}, bf16[512,128]{0,1:T(8,128)(2,1)S(1)}, u32[]{:S(2)}, u32[]{:S(2)}) collective-permute-start(bf16[512,128]{0,1:T(8,128)(2,1)S(1)} %get-tuple-element.12), channel_id=1, source_target_pairs={{0,1},{1,2},{2,3},{3,4},{4,5},{5,6},{6,7},{8,9},{9,10},{10,11},{11... | collective-permute-start | bytes 393224 | tf_op jit(solution)/shard_map/ppermute | solution.py:16
  61.2 1.6 copy.19
  64.4 3.7 %fusion.52 = f32[8,128,512]{2,1,0:T(8,128)S(1)} fusion(bf16[8,512,128]{2,1,0:T(8,128)(2,1)S(1)} %bitcast.133, bf16[8,512,512]{2,1,0:T(8,128)(2,1)} %param.7), kind=kOutput, calls=%fused_computation.62 | convolution fusion | flops 536870912 | bytes 7340032 | tf_op jit(solution)/shard_map/bij,bjk->bik/dot_general | solution.py:35
  68.1 7.6 %fusion.35 = bf16[8,512,128]{1,2,0:T(8,128)(2,1)} fusion(bf16[1,8,512,512]{3,2,1,0:T(8,128)(2,1)} %param.6, bf16[8,512,128]{1,2,0:T(8,128)(2,1)S(1)} %copy.15, f32[8,128,512]{2,1,0:T(8,128)S(1)} %fusion.52, bf16[8,512,128]{2,1,0:T(8,128)(2,1)} %bitcast.140, bf16[8,512,512]{2,1,0:T(8,128)(2,1)} %param.8), kind=kOutput, calls=%fused_computation.28 | convolution fusion | flops 1076363264 | bytes 13631488 | tf_op jit(solution)/shard_map/bij,bjk->bik/dot_general | solution.py:41
  76.7 5.0 %collective-permute-start.6 = (bf16[512,128]{0,1:T(8,128)(2,1)S(1)}, bf16[512,128]{0,1:T(8,128)(2,1)S(1)}, u32[]{:S(2)}, u32[]{:S(2)}) collective-permute-start(bf16[512,128]{0,1:T(8,128)(2,1)S(1)} %get-tuple-element.8), channel_id=1, source_target_pairs={{0,1},{1,2},{2,3},{3,4},{4,5},{5,6},{6,7},{8,9},{9,10},{10,11},{11... | collective-permute-start | bytes 393224 | tf_op jit(solution)/shard_map/ppermute | solution.py:16
  86.9 3.7 %fusion.53 = f32[8,128,512]{2,1,0:T(8,128)S(1)} fusion(bf16[8,512,128]{2,1,0:T(8,128)(2,1)S(1)} %bitcast.134, bf16[8,512,512]{2,1,0:T(8,128)(2,1)} %param.7), kind=kOutput, calls=%fused_computation.63 | convolution fusion | flops 536870912 | bytes 7340032 | tf_op jit(solution)/shard_map/bij,bjk->bik/dot_general | solution.py:35
  90.6 8.0 %multiply_bitcast_fusion = f32[8,512,128]{1,2,0:T(8,128)} fusion(bf16[1,8,512,512]{3,2,1,0:T(8,128)(2,1)} %param.6, bf16[8,512,128]{1,2,0:T(8,128)(2,1)S(1)} %copy.15, f32[8,128,512]{2,1,0:T(8,128)S(1)} %fusion.53, bf16[8,512,128]{2,1,0:T(8,128)(2,1)} %bitcast.130, bf16[8,512,512]{2,1,0:T(8,128)(2,1)} %param.8, f32[]{:T(128)} %bitcast.128), kind=kOutput, calls=%fused_computation.22 | convolution fusion | flops 1077411840 | bytes 14680068 | tf_op jit(solution)/shard_map/bij,bjk->bik/dot_general | solution.py:41
  98.5 2.9 %copy.25 = f32[8,512,128]{2,1,0:T(8,128)} copy(f32[8,512,128]{1,2,0:T(8,128)} %multiply_bitcast_fusion) | data formatting | bytes 4194304 | tf_op jit(solution)/shard_map/mul | solution.py:44
  101.5 71.8 %all-reduce.3.cloned.1.call-done = f32[4096,128]{1,0:T(8,128)} async-done(((f32[4096,128]{1,0:T(8,128)}), f32[4096,128]{1,0:T(8,128)}) %all-reduce.3.cloned.1.call-update) | async-done | bytes 2097168 | tf_op jit(solution)/shard_map/psum | solution.py:46
  173.4 6.3 %fusion.54 = f32[128,128]{0,1:T(8,128)} fusion(f32[4096,128]{1,0:T(8,128)} %all-reduce.3.cloned.1.call-done), kind=kOutput, calls=%fused_computation.64 | convolution fusion | flops 805306368 | bytes 2162688 | tf_op jit(solution)/shard_map/dot_general | solution.py:49
  179.7 54.8 %all-reduce.5.cloned.1.call-done = f32[128,128]{0,1:T(8,128)} async-done(((f32[128,128]{0,1:T(8,128)}), f32[128,128]{0,1:T(8,128)}) %all-reduce.5.cloned.1.call-update) | async-done | bytes 65552 | tf_op jit(solution)/shard_map/psum | solution.py:50
  236.3 11.7 %cholesky.16 = f32[128,128]{1,0:T(8,128)S(1)} custom-call(f32[128,128]{1,0:T(8,128)S(1)} %fusion.48), custom_call_target="Cholesky" | custom-call | tf_op jit(solution)/shard_map/jit(cholesky)/cholesky | solution.py:52
  249.4 9.8 %custom-call.7 = f32[1,128,128]{1,2,0:T(8,128)S(1)} custom-call(f32[1,128,128]{2,1,0:T(8,128)S(1)} %fusion.46), custom_call_target="InvertDiagBlocksLowerTriangular" | custom-call | tf_op jit(solution)/shard_map/jit(_solve_triangular)/triangular_solve | solution.py:53
  259.2 2.4 fusion.44
  (38 shorter events, 18.1 us)
Async XLA Ops:
  6.5 166.8 %all-reduce.3.cloned.1.call-start = ((), (), s32[]{:S(2)}) async-start(), calls=%async_computation | async-start | bytes 4194304 | tf_op jit(solution)/shard_map/psum | solution.py:46
  6.5 7.6 %copy-start = (bf16[4096,128]{1,0:T(8,128)(2,1)S(1)}, bf16[4096,128]{1,0:T(8,128)(2,1)}, u32[]{:S(2)}) copy-start(bf16[4096,128]{1,0:T(8,128)(2,1)} %param.5) | copy-start | bytes 3145732
  10.4 4.3 %collective-permute-start = (bf16[512,128]{1,0:T(8,128)(2,1)S(1)}, bf16[512,128]{1,0:T(8,128)(2,1)S(1)}, u32[]{:S(2)}, u32[]{:S(2)}) collective-permute-start(bf16[512,128]{1,0:T(8,128)(2,1)S(1)} %get-tuple-element.20), channel_id=1, source_target_pairs={{0,1},{1,2},{2,3},{3,4},{4,5},{5,6},{6,7},{8,9},{9,10},{10,11},{11... | collective-permute-start | bytes 393224 | tf_op jit(solution)/shard_map/ppermute | solution.py:16
  12.8 5.5 %collective-permute-start.1 = (bf16[512,128]{1,0:T(8,128)(2,1)S(1)}, bf16[512,128]{1,0:T(8,128)(2,1)}, u32[]{:S(2)}, u32[]{:S(2)}) collective-permute-start(bf16[512,128]{1,0:T(8,128)(2,1)S(1)} %get-tuple-element.19), channel_id=1, source_target_pairs={{1,0},{2,1},{3,2},{4,3},{5,4},{6,5},{7,6},{9,8},{10,9},{11,10},{12... | collective-permute-start | bytes 393224 | tf_op jit(solution)/shard_map/ppermute | solution.py:17
  32.7 8.4 %collective-permute-start.2 = (bf16[512,128]{0,1:T(8,128)(2,1)S(1)}, bf16[512,128]{0,1:T(8,128)(2,1)S(1)}, u32[]{:S(2)}, u32[]{:S(2)}) collective-permute-start(bf16[512,128]{0,1:T(8,128)(2,1)S(1)} %get-tuple-element.16), channel_id=1, source_target_pairs={{0,1},{1,2},{2,3},{3,4},{4,5},{5,6},{6,7},{8,9},{9,10},{10,11},{11... | collective-permute-start | bytes 393224 | tf_op jit(solution)/shard_map/ppermute | solution.py:16
  38.1 3.2 %collective-permute-start.3 = (bf16[512,128]{0,1:T(8,128)(2,1)S(1)}, bf16[512,128]{0,1:T(8,128)(2,1)S(1)}, u32[]{:S(2)}, u32[]{:S(2)}) collective-permute-start(bf16[512,128]{0,1:T(8,128)(2,1)S(1)} %get-tuple-element.15), channel_id=1, source_target_pairs={{1,0},{2,1},{3,2},{4,3},{5,4},{6,5},{7,6},{9,8},{10,9},{11,10},{12... | collective-permute-start | bytes 393224 | tf_op jit(solution)/shard_map/ppermute | solution.py:17
  55.0 7.9 %collective-permute-start.4 = (bf16[512,128]{0,1:T(8,128)(2,1)S(1)}, bf16[512,128]{0,1:T(8,128)(2,1)S(1)}, u32[]{:S(2)}, u32[]{:S(2)}) collective-permute-start(bf16[512,128]{0,1:T(8,128)(2,1)S(1)} %get-tuple-element.12), channel_id=1, source_target_pairs={{0,1},{1,2},{2,3},{3,4},{4,5},{5,6},{6,7},{8,9},{9,10},{10,11},{11... | collective-permute-start | bytes 393224 | tf_op jit(solution)/shard_map/ppermute | solution.py:16
  59.9 3.2 %collective-permute-start.5 = (bf16[512,128]{0,1:T(8,128)(2,1)S(1)}, bf16[512,128]{0,1:T(8,128)(2,1)S(1)}, u32[]{:S(2)}, u32[]{:S(2)}) collective-permute-start(bf16[512,128]{0,1:T(8,128)(2,1)S(1)} %get-tuple-element.11), channel_id=1, source_target_pairs={{1,0},{2,1},{3,2},{4,3},{5,4},{6,5},{7,6},{9,8},{10,9},{11,10},{12... | collective-permute-start | bytes 393224 | tf_op jit(solution)/shard_map/ppermute | solution.py:17
  76.7 8.7 %collective-permute-start.6 = (bf16[512,128]{0,1:T(8,128)(2,1)S(1)}, bf16[512,128]{0,1:T(8,128)(2,1)S(1)}, u32[]{:S(2)}, u32[]{:S(2)}) collective-permute-start(bf16[512,128]{0,1:T(8,128)(2,1)S(1)} %get-tuple-element.8), channel_id=1, source_target_pairs={{0,1},{1,2},{2,3},{3,4},{4,5},{5,6},{6,7},{8,9},{9,10},{10,11},{11... | collective-permute-start | bytes 393224 | tf_op jit(solution)/shard_map/ppermute | solution.py:16
  81.7 3.9 %collective-permute-start.7 = (bf16[512,128]{0,1:T(8,128)(2,1)S(1)}, bf16[512,128]{0,1:T(8,128)(2,1)S(1)}, u32[]{:S(2)}, u32[]{:S(2)}) collective-permute-start(bf16[512,128]{0,1:T(8,128)(2,1)S(1)} %get-tuple-element.7), channel_id=1, source_target_pairs={{1,0},{2,1},{3,2},{4,3},{5,4},{6,5},{7,6},{9,8},{10,9},{11,10},{12... | collective-permute-start | bytes 393224 | tf_op jit(solution)/shard_map/ppermute | solution.py:17
  101.5 133.1 %all-reduce.5.cloned.1.call-start = ((), (), s32[]{:S(2)}) async-start(), calls=%async_computation.1 | async-start | bytes 131072 | tf_op jit(solution)/shard_map/psum | solution.py:50
Sparse Core Ops, SparseCore 0:
  101.6 71.7 all-reduce.2
  179.8 54.6 all-reduce.4
where the time goes:
time: 269 us; the launch traced here: 268 us
  waiting for transfers between devices  131 us (49%)
  matrix products  58.2 us (22%)
  other arithmetic  29.9 us (11%)
  starting transfers between devices  23.2 us (9%)
  between operations  14.3 us (5%)
  local copies, waits for them, and re-layouts  12.1 us (4%)
    psum x1, waiting for transfers between devices, shards(): filtered = lax.psum(weighted, 'pole')  71.8 us
    psum x1, waiting for transfers between devices, shards(): gram = lax.psum(partial_gram, 'row')  54.8 us
    dot_general x4, matrix products, shards(): jnp.einsum('bij,bjk->bik', inverse, rhs.astype(jnp.bfloat16), preferred_e...  30.9 us
    ppermute x4, starting transfers between devices, padded_2(): before = lax.ppermute(last, axis, up)  17.8 us
    dot_general x4, matrix products, shards(): jnp.einsum('bij,bjk->bik', lower, padded[:-2], preferred_element_type=jnp...  14.8 us
    another operation x3, other arithmetic, shards(): factor = jnp.linalg.cholesky(gram)  12.4 us
    another operation x2, other arithmetic, shards(): solved = jax.scipy.linalg.solve_triangular(factor, mine.T, lower=True)  10.5 us
    dot_general x1, matrix products, shards(): jnp.dot(filtered.T, filtered, precision=lax.Precision.HIGHEST)  6.31 us
  transfers between devices with their start and end apart: 10, of which 5 were waited for; matrix products, arithmetic and copies ran while one was open for 2% of the time, Pallas kernels for 0%

commit v1 on v0

--- a/solution.py
+++ b/solution.py
@@ -43,7 +43,9 @@
         ).astype(jnp.bfloat16)
     weighted = pole_weights[0] * state.reshape(rows, width).astype(jnp.float32)
     total_rows = rows * lax.axis_size("row")
-    filtered = lax.psum(weighted, "pole")
+    filtered = weighted
+    for hop in (1, 2):
+        filtered = filtered + lax.ppermute(filtered, "pole", [(dev, dev ^ hop) for dev in range(4)])
     share = rows // lax.axis_size("pole")
     mine = lax.dynamic_slice_in_dim(filtered, lax.axis_index("pole") * share, share, 0)
     partial_gram = jnp.dot(filtered.T, filtered, precision=lax.Precision.HIGHEST)

time: 269 us -> 290 us (1.078)
  waiting for transfers between devices: 131 us -> 153 us
  matrix products: 58.2 us -> 55 us
  starting transfers between devices: 23.2 us -> 26.3 us
    ppermute x0 -> x2, waiting for transfers between devices: none -> 92.3 us  [shards(): lax.ppermute(filtered, 'pole', [(dev, dev ^ hop) for dev in range(4)])]
    psum x1 -> x0, waiting for transfers between devices: 71.8 us -> none  [shards(): filtered = lax.psum(weighted, 'pole')]
    ppermute x0 -> x2, starting transfers between devices: none -> 3.14 us  [shards(): lax.ppermute(filtered, 'pole', [(dev, dev ^ hop) for dev in range(4)])]
  transfers between devices with their start and end apart: 10 -> 11, of which waited for: 5 -> 6; matrix products, arithmetic and copies ran while one was open for 2% -> 2% of each run, Pallas kernels for 0% -> 0%
where the time goes in v1:
time: 290 us
  waiting for transfers between devices  153 us (53%)
  matrix products  55 us (19%)
  other arithmetic  30.4 us (10%)
  starting transfers between devices  26.3 us (9%)
  between operations  14.3 us (5%)
  local copies, waits for them, and re-layouts  11.1 us (4%)
    ppermute x2, waiting for transfers between devices, shards(): lax.ppermute(filtered, 'pole', [(dev, dev ^ hop) for dev in range(4)])  92.3 us
    psum x1, waiting for transfers between devices, shards(): gram = lax.psum(partial_gram, 'row')  56.3 us
    dot_general x4, matrix products, shards(): jnp.einsum('bij,bjk->bik', inverse, rhs.astype(jnp.bfloat16), preferred_e...  30.9 us
    ppermute x4, starting transfers between devices, padded_2(): before = lax.ppermute(last, axis, up)  17.8 us
    dot_general x4, matrix products, shards(): jnp.einsum('bij,bjk->bik', lower, padded[:-2], preferred_element_type=jnp...  14.8 us
    another operation x3, other arithmetic, shards(): factor = jnp.linalg.cholesky(gram)  12.4 us
    another operation x2, other arithmetic, shards(): solved = jax.scipy.linalg.solve_triangular(factor, mine.T, lower=True)  10.5 us
  transfers between devices with their start and end apart: 11, of which 6 were waited for; matrix products, arithmetic and copies ran while one was open for 2% of the time, Pallas kernels for 0%

profile of v1, /device:TPU:0, one launch (start us, length us, event | category | flops | bytes accessed | tf_op | source)
XLA Modules:
  0.0 289.6 jit_solution(17731752168820075530)
XLA Ops:
  6.5 3.8 %fusion.18 = bf16[8,512,128]{2,1,0:T(8,128)(2,1)S(1)} fusion(bf16[8,512,128]{2,1,0:T(8,128)(2,1)} %bitcast.143, bf16[1,8,512,512]{3,2,1,0:T(8,128)(2,1)} %param.6), kind=kOutput, calls=%fused_computation.23 | convolution fusion | flops 537395200 | bytes 6291456 | tf_op jit(solution)/shard_map/bij,bjk->bik/dot_general | solution.py:28
  10.4 2.4 collective-permute-start
  14.7 3.7 %collective-permute-done.1 = bf16[512,128]{1,0:T(8,128)(2,1)} collective-permute-done((bf16[512,128]{1,0:T(8,128)(2,1)S(1)}, bf16[512,128]{1,0:T(8,128)(2,1)}, u32[]{:S(2)}, u32[]{:S(2)}) %collective-permute-start.1) | collective-permute-done | bytes 131104 | tf_op jit(solution)/shard_map/ppermute | solution.py:17
  18.4 2.0 pad_maximum_fusion.6
  20.4 3.7 %fusion.50 = f32[8,128,512]{2,1,0:T(8,128)S(1)} fusion(bf16[8,512,128]{2,1,0:T(8,128)(2,1)S(1)} %bitcast.132, bf16[8,512,512]{2,1,0:T(8,128)(2,1)} %param.7), kind=kOutput, calls=%fused_computation.61 | convolution fusion | flops 536870912 | bytes 7340032 | tf_op jit(solution)/shard_map/bij,bjk->bik/dot_general | solution.py:35
  24.1 7.6 %fusion.41 = bf16[8,512,128]{1,2,0:T(8,128)(2,1)} fusion(bf16[1,8,512,512]{3,2,1,0:T(8,128)(2,1)} %param.6, bf16[8,512,128]{1,2,0:T(8,128)(2,1)S(1)} %copy.15, f32[8,128,512]{2,1,0:T(8,128)S(1)} %fusion.50, bf16[8,512,128]{2,1,0:T(8,128)(2,1)} %bitcast.139, bf16[8,512,512]{2,1,0:T(8,128)(2,1)} %param.8), kind=kOutput, calls=%fused_computation.30 | convolution fusion | flops 1076363264 | bytes 13631488 | tf_op jit(solution)/shard_map/bij,bjk->bik/dot_general | solution.py:41
  32.7 5.4 %collective-permute-start.2 = (bf16[512,128]{0,1:T(8,128)(2,1)S(1)}, bf16[512,128]{0,1:T(8,128)(2,1)S(1)}, u32[]{:S(2)}, u32[]{:S(2)}) collective-permute-start(bf16[512,128]{0,1:T(8,128)(2,1)S(1)} %get-tuple-element.16), channel_id=1, source_target_pairs={{0,1},{1,2},{2,3},{3,4},{4,5},{5,6},{6,7},{8,9},{9,10},{10,11},{11... | collective-permute-start | bytes 393224 | tf_op jit(solution)/shard_map/ppermute | solution.py:16
  39.4 1.6 copy.16
  42.6 3.7 %fusion.51 = f32[8,128,512]{2,1,0:T(8,128)S(1)} fusion(bf16[8,512,128]{2,1,0:T(8,128)(2,1)S(1)} %bitcast.133, bf16[8,512,512]{2,1,0:T(8,128)(2,1)} %param.7), kind=kOutput, calls=%fused_computation.62 | convolution fusion | flops 536870912 | bytes 7340032 | tf_op jit(solution)/shard_map/bij,bjk->bik/dot_general | solution.py:35
  46.3 7.6 %fusion.38 = bf16[8,512,128]{1,2,0:T(8,128)(2,1)} fusion(bf16[1,8,512,512]{3,2,1,0:T(8,128)(2,1)} %param.6, bf16[8,512,128]{1,2,0:T(8,128)(2,1)S(1)} %copy.15, f32[8,128,512]{2,1,0:T(8,128)S(1)} %fusion.51, bf16[8,512,128]{2,1,0:T(8,128)(2,1)} %bitcast.140, bf16[8,512,512]{2,1,0:T(8,128)(2,1)} %param.8), kind=kOutput, calls=%fused_computation.29 | convolution fusion | flops 1076363264 | bytes 13631488 | tf_op jit(solution)/shard_map/bij,bjk->bik/dot_general | solution.py:41
  55.0 5.0 %collective-permute-start.4 = (bf16[512,128]{0,1:T(8,128)(2,1)S(1)}, bf16[512,128]{0,1:T(8,128)(2,1)S(1)}, u32[]{:S(2)}, u32[]{:S(2)}) collective-permute-start(bf16[512,128]{0,1:T(8,128)(2,1)S(1)} %get-tuple-element.12), channel_id=1, source_target_pairs={{0,1},{1,2},{2,3},{3,4},{4,5},{5,6},{6,7},{8,9},{9,10},{10,11},{11... | collective-permute-start | bytes 393224 | tf_op jit(solution)/shard_map/ppermute | solution.py:16
  61.2 1.6 copy.19
  64.4 3.7 %fusion.52 = f32[8,128,512]{2,1,0:T(8,128)S(1)} fusion(bf16[8,512,128]{2,1,0:T(8,128)(2,1)S(1)} %bitcast.134, bf16[8,512,512]{2,1,0:T(8,128)(2,1)} %param.7), kind=kOutput, calls=%fused_computation.63 | convolution fusion | flops 536870912 | bytes 7340032 | tf_op jit(solution)/shard_map/bij,bjk->bik/dot_general | solution.py:35
  68.1 7.6 %fusion.35 = bf16[8,512,128]{1,2,0:T(8,128)(2,1)} fusion(bf16[1,8,512,512]{3,2,1,0:T(8,128)(2,1)} %param.6, bf16[8,512,128]{1,2,0:T(8,128)(2,1)S(1)} %copy.15, f32[8,128,512]{2,1,0:T(8,128)S(1)} %fusion.52, bf16[8,512,128]{2,1,0:T(8,128)(2,1)} %bitcast.141, bf16[8,512,512]{2,1,0:T(8,128)(2,1)} %param.8), kind=kOutput, calls=%fused_computation.28 | convolution fusion | flops 1076363264 | bytes 13631488 | tf_op jit(solution)/shard_map/bij,bjk->bik/dot_general | solution.py:41
  76.7 5.0 %collective-permute-start.6 = (bf16[512,128]{0,1:T(8,128)(2,1)S(1)}, bf16[512,128]{0,1:T(8,128)(2,1)S(1)}, u32[]{:S(2)}, u32[]{:S(2)}) collective-permute-start(bf16[512,128]{0,1:T(8,128)(2,1)S(1)} %get-tuple-element.8), channel_id=1, source_target_pairs={{0,1},{1,2},{2,3},{3,4},{4,5},{5,6},{6,7},{8,9},{9,10},{10,11},{11... | collective-permute-start | bytes 393224 | tf_op jit(solution)/shard_map/ppermute | solution.py:16
  86.8 3.7 %fusion.53 = f32[8,128,512]{2,1,0:T(8,128)S(1)} fusion(bf16[8,512,128]{2,1,0:T(8,128)(2,1)S(1)} %bitcast.135, bf16[8,512,512]{2,1,0:T(8,128)(2,1)} %param.7), kind=kOutput, calls=%fused_computation.64 | convolution fusion | flops 536870912 | bytes 7340032 | tf_op jit(solution)/shard_map/bij,bjk->bik/dot_general | solution.py:35
  90.5 8.0 %multiply_bitcast_fusion = f32[8,512,128]{1,2,0:T(8,128)} fusion(bf16[1,8,512,512]{3,2,1,0:T(8,128)(2,1)} %param.6, bf16[8,512,128]{1,2,0:T(8,128)(2,1)S(1)} %copy.15, f32[8,128,512]{2,1,0:T(8,128)S(1)} %fusion.53, bf16[8,512,128]{2,1,0:T(8,128)(2,1)} %bitcast.131, bf16[8,512,512]{2,1,0:T(8,128)(2,1)} %param.8, f32[]{:T(128)} %bitcast.129), kind=kOutput, calls=%fused_computation.22 | convolution fusion | flops 1077411840 | bytes 14680068 | tf_op jit(solution)/shard_map/bij,bjk->bik/dot_general | solution.py:41
  98.5 1.9 copy.25
  102.0 45.6 %collective-permute-done.8 = f32[4096,128]{1,0:T(8,128)S(1)} collective-permute-done((f32[4096,128]{1,0:T(8,128)S(1)}, f32[4096,128]{1,0:T(8,128)S(1)}, u32[]{:S(2)}, u32[]{:S(2)}) %collective-permute-start.8) | collective-permute-done | bytes 2097184 | tf_op jit(solution)/shard_map/ppermute | solution.py:48
  149.4 46.7 %collective-permute-done.9 = f32[4096,128]{1,0:T(8,128)S(1)} collective-permute-done((f32[4096,128]{1,0:T(8,128)S(1)}, f32[4096,128]{1,0:T(8,128)S(1)}, u32[]{:S(2)}, u32[]{:S(2)}) %collective-permute-start.9) | collective-permute-done | bytes 2097184 | tf_op jit(solution)/shard_map/ppermute | solution.py:48
  196.4 4.1 %fusion.54 = f32[128,128]{0,1:T(8,128)} fusion(f32[4096,128]{1,0:T(8,128)S(1)} %add.56), kind=kOutput, calls=%fused_computation.65 | convolution fusion | flops 805306368 | bytes 2162688 | tf_op jit(solution)/shard_map/dot_general | solution.py:51
  200.5 56.3 %all-reduce.2.cloned.1.call-done = f32[128,128]{0,1:T(8,128)} async-done(((f32[128,128]{0,1:T(8,128)}), f32[128,128]{0,1:T(8,128)}) %all-reduce.2.cloned.1.call-update) | async-done | bytes 65552 | tf_op jit(solution)/shard_map/psum | solution.py:52
  258.6 11.7 %cholesky.16 = f32[128,128]{1,0:T(8,128)S(1)} custom-call(f32[128,128]{1,0:T(8,128)S(1)} %fusion.48), custom_call_target="Cholesky" | custom-call | tf_op jit(solution)/shard_map/jit(cholesky)/cholesky | solution.py:54
  271.6 9.8 %custom-call.7 = f32[1,128,128]{1,2,0:T(8,128)S(1)} custom-call(f32[1,128,128]{2,1,0:T(8,128)S(1)} %fusion.46), custom_call_target="InvertDiagBlocksLowerTriangular" | custom-call | tf_op jit(solution)/shard_map/jit(_solve_triangular)/triangular_solve | solution.py:55
  (41 shorter events, 23.0 us)
Async XLA Ops:
  6.5 250.2 %all-reduce.2.cloned.1.call-start = ((), (), s32[]{:S(2)}) async-start(), calls=%async_computation | async-start | bytes 131072 | tf_op jit(solution)/shard_map/psum | solution.py:52
  6.5 7.6 %copy-start = (bf16[4096,128]{1,0:T(8,128)(2,1)S(1)}, bf16[4096,128]{1,0:T(8,128)(2,1)}, u32[]{:S(2)}) copy-start(bf16[4096,128]{1,0:T(8,128)(2,1)} %param.5) | copy-start | bytes 3145732
  10.4 4.3 %collective-permute-start = (bf16[512,128]{1,0:T(8,128)(2,1)S(1)}, bf16[512,128]{1,0:T(8,128)(2,1)S(1)}, u32[]{:S(2)}, u32[]{:S(2)}) collective-permute-start(bf16[512,128]{1,0:T(8,128)(2,1)S(1)} %get-tuple-element.20), channel_id=1, source_target_pairs={{0,1},{1,2},{2,3},{3,4},{4,5},{5,6},{6,7},{8,9},{9,10},{10,11},{11... | collective-permute-start | bytes 393224 | tf_op jit(solution)/shard_map/ppermute | solution.py:16
  12.8 5.5 %collective-permute-start.1 = (bf16[512,128]{1,0:T(8,128)(2,1)S(1)}, bf16[512,128]{1,0:T(8,128)(2,1)}, u32[]{:S(2)}, u32[]{:S(2)}) collective-permute-start(bf16[512,128]{1,0:T(8,128)(2,1)S(1)} %get-tuple-element.19), channel_id=1, source_target_pairs={{1,0},{2,1},{3,2},{4,3},{5,4},{6,5},{7,6},{9,8},{10,9},{11,10},{12... | collective-permute-start | bytes 393224 | tf_op jit(solution)/shard_map/ppermute | solution.py:17
  32.7 8.4 %collective-permute-start.2 = (bf16[512,128]{0,1:T(8,128)(2,1)S(1)}, bf16[512,128]{0,1:T(8,128)(2,1)S(1)}, u32[]{:S(2)}, u32[]{:S(2)}) collective-permute-start(bf16[512,128]{0,1:T(8,128)(2,1)S(1)} %get-tuple-element.16), channel_id=1, source_target_pairs={{0,1},{1,2},{2,3},{3,4},{4,5},{5,6},{6,7},{8,9},{9,10},{10,11},{11... | collective-permute-start | bytes 393224 | tf_op jit(solution)/shard_map/ppermute | solution.py:16
  38.1 3.2 %collective-permute-start.3 = (bf16[512,128]{0,1:T(8,128)(2,1)S(1)}, bf16[512,128]{0,1:T(8,128)(2,1)S(1)}, u32[]{:S(2)}, u32[]{:S(2)}) collective-permute-start(bf16[512,128]{0,1:T(8,128)(2,1)S(1)} %get-tuple-element.15), channel_id=1, source_target_pairs={{1,0},{2,1},{3,2},{4,3},{5,4},{6,5},{7,6},{9,8},{10,9},{11,10},{12... | collective-permute-start | bytes 393224 | tf_op jit(solution)/shard_map/ppermute | solution.py:17
  55.0 7.9 %collective-permute-start.4 = (bf16[512,128]{0,1:T(8,128)(2,1)S(1)}, bf16[512,128]{0,1:T(8,128)(2,1)S(1)}, u32[]{:S(2)}, u32[]{:S(2)}) collective-permute-start(bf16[512,128]{0,1:T(8,128)(2,1)S(1)} %get-tuple-element.12), channel_id=1, source_target_pairs={{0,1},{1,2},{2,3},{3,4},{4,5},{5,6},{6,7},{8,9},{9,10},{10,11},{11... | collective-permute-start | bytes 393224 | tf_op jit(solution)/shard_map/ppermute | solution.py:16
  59.9 3.2 %collective-permute-start.5 = (bf16[512,128]{0,1:T(8,128)(2,1)S(1)}, bf16[512,128]{0,1:T(8,128)(2,1)S(1)}, u32[]{:S(2)}, u32[]{:S(2)}) collective-permute-start(bf16[512,128]{0,1:T(8,128)(2,1)S(1)} %get-tuple-element.11), channel_id=1, source_target_pairs={{1,0},{2,1},{3,2},{4,3},{5,4},{6,5},{7,6},{9,8},{10,9},{11,10},{12... | collective-permute-start | bytes 393224 | tf_op jit(solution)/shard_map/ppermute | solution.py:17
  76.7 8.7 %collective-permute-start.6 = (bf16[512,128]{0,1:T(8,128)(2,1)S(1)}, bf16[512,128]{0,1:T(8,128)(2,1)S(1)}, u32[]{:S(2)}, u32[]{:S(2)}) collective-permute-start(bf16[512,128]{0,1:T(8,128)(2,1)S(1)} %get-tuple-element.8), channel_id=1, source_target_pairs={{0,1},{1,2},{2,3},{3,4},{4,5},{5,6},{6,7},{8,9},{9,10},{10,11},{11... | collective-permute-start | bytes 393224 | tf_op jit(solution)/shard_map/ppermute | solution.py:16
  81.7 3.9 %collective-permute-start.7 = (bf16[512,128]{0,1:T(8,128)(2,1)S(1)}, bf16[512,128]{0,1:T(8,128)(2,1)S(1)}, u32[]{:S(2)}, u32[]{:S(2)}) collective-permute-start(bf16[512,128]{0,1:T(8,128)(2,1)S(1)} %get-tuple-element.7), channel_id=1, source_target_pairs={{1,0},{2,1},{3,2},{4,3},{5,4},{6,5},{7,6},{9,8},{10,9},{11,10},{12... | collective-permute-start | bytes 393224 | tf_op jit(solution)/shard_map/ppermute | solution.py:17
  100.4 47.1 %collective-permute-start.8 = (f32[4096,128]{1,0:T(8,128)S(1)}, f32[4096,128]{1,0:T(8,128)S(1)}, u32[]{:S(2)}, u32[]{:S(2)}) collective-permute-start(f32[4096,128]{1,0:T(8,128)S(1)} %bitcast.130), channel_id=1, source_target_pairs={{0,8},{8,0},{16,24},{24,16},{1,9},{9,1},{17,25},{25,17},{2,10},{10... | collective-permute-start | bytes 6291464 | tf_op jit(solution)/shard_map/ppermute | solution.py:48
  147.8 48.3 %collective-permute-start.9 = (f32[4096,128]{1,0:T(8,128)S(1)}, f32[4096,128]{1,0:T(8,128)S(1)}, u32[]{:S(2)}, u32[]{:S(2)}) collective-permute-start(f32[4096,128]{1,0:T(8,128)S(1)} %bitcast_add_fusion.1), channel_id=1, source_target_pairs={{0,16},{8,24},{16,0},{24,8},{1,17},{9,25},{17,1},{25,9},{2,18},{10... | collective-permute-start | bytes 6291464 | tf_op jit(solution)/shard_map/ppermute | solution.py:48
Sparse Core Ops, SparseCore 0:
  200.6 56.1 all-reduce.1
